TPU v7x, 32 devices: a whole 2x2x4 slice. The times are simulated.
32 devices in a mesh: scen: 4 (over y, core), row: 8 (over z, x).
Axes of the slice: x: 2, y: 2, z: 4, core: 2. Of those that a mesh axis runs over, the one named last changes fastest.
Arguments:
- borders: bfloat16 [4, 1024, 12288], P('scen', None, 'row'), may hold values from -1.078125 to 1.078125
- kkt_inverse: bfloat16 [4, 1024, 1024], P('scen', 'row'), may hold values from -0.35 to 2.35, as said below
- first_section: float32 [12288, 256], P('row'), may hold values from -6 to 6
- barrier: float32 [12288], P('row'), may hold values from 64 to 512
- panel_vars: int32 [256], replicated, may hold values from 0 to 12287, as said below
- probability: float32 [4], replicated, may hold values from 0.5 to 2
- assignment: int32 [4], P('scen'), may hold values from 0 to 3, each once
Outputs:
- factor: float32 [12288, 256], P('row')
Inputs may be any that keep to these rules, and one draw needn't show every extreme that they name: `panel_vars`: distinct values. `kkt_inverse`: each scenario's matrix is symmetric positive definite. `assignment`: each scenario once.
All inputs are finite; a program needn't handle non-finite values.
Results may differ from a plain program's by a relative error of at most 0.00031.
Values may be sent and summed in bfloat16 or wider, within the bound.
A program may use at most 64 MiB of HBM per device.

v0:
```python
import jax
import jax.numpy as jnp
from jax import lax
from jax.sharding import PartitionSpec as P

PANEL = 128
PANELS = 2


def factorize(diag_block, row_block):
    symmetric = 0.5 * (diag_block + diag_block.T)
    block_parts = []
    row_parts = []
    for panel_index in range(PANELS):
        low_col = panel_index * PANEL
        high_col = low_col + PANEL
        block_cols = symmetric[:, low_col:high_col]
        row_cols = row_block[:, low_col:high_col]
        if panel_index > 0:
            earlier_block = block_parts[0]
            earlier_rows = row_parts[0]
            across = earlier_block[low_col:high_col, :]
            block_cols = block_cols - jnp.dot(
                earlier_block, across.T, precision=lax.Precision.HIGHEST
            )
            row_cols = row_cols - jnp.dot(earlier_rows, across.T, precision=lax.Precision.HIGHEST)
        panel_chol = jnp.linalg.cholesky(block_cols[low_col:high_col, :])
        block_parts.append(
            lax.linalg.triangular_solve(
                panel_chol, block_cols, left_side=False, lower=True, transpose_a=True
            )
        )
        row_parts.append(
            lax.linalg.triangular_solve(
                panel_chol, row_cols, left_side=False, lower=True, transpose_a=True
            )
        )
    return jnp.concatenate(row_parts, axis=1)


def per_device(borders, kkt_inverse, first_section, barrier, panel_vars, probability, assignment):
    rows_dev = first_section.shape[0]
    first_row = lax.axis_index("row") * rows_dev
    local_index = panel_vars - first_row
    inside = (local_index >= 0) & (local_index < rows_dev)
    clipped = jnp.clip(local_index, 0, rows_dev - 1)
    picked = jnp.take(borders, clipped, axis=2) * inside.astype(jnp.bfloat16)[None, None, :]
    columns = lax.psum(picked, "row").astype(jnp.float32).astype(jnp.bfloat16)
    own_solved = jnp.einsum(
        "sij,sjc->sic", kkt_inverse, columns, preferred_element_type=jnp.float32
    ).astype(jnp.bfloat16)
    solved = lax.all_gather(own_solved, "row", axis=1, tiled=True)
    scen_count = probability.shape[0]
    matches = assignment[:, None] == jnp.arange(scen_count, dtype=jnp.int32)[None, :]
    weight = jnp.sum(jnp.where(matches, probability[None, :], 0.0), axis=1)
    leading = (lax.axis_index("scen") == 0).astype(jnp.float32)
    hits = jnp.arange(rows_dev, dtype=jnp.int32)[:, None] + first_row == panel_vars[None, :]
    baseline = first_section + jnp.where(hits, barrier[:, None], 0.0)
    term = jnp.einsum("snr,snc->src", borders, solved, preferred_element_type=jnp.float32)
    contribution = jnp.sum(term * weight[:, None, None], axis=0) + leading * baseline
    own_block = jnp.take(contribution, clipped, axis=0) * inside.astype(jnp.float32)[:, None]
    diag_block = lax.psum(own_block, ("scen", "row"))
    schur = lax.psum(contribution, "scen")
    factor = factorize(diag_block, schur)
    return factor


def solution(mesh):
    placed = (
        P("scen", None, "row"),
        P("scen", "row", None),
        P("row", None),
        P("row"),
        P(),
        P(),
        P("scen"),
    )
    return jax.shard_map(
        per_device, mesh=mesh, in_specs=placed, out_specs=P("row", None), check_vma=False
    )
```

profile of v0, /device:TPU:0, one launch (start us, length us, event | category | flops | bytes accessed | tf_op | source)
XLA Modules:
  0.0 313.0 jit_solution(12888756615354022257)
XLA Ops:
  6.5 0.0 copy-start
  6.5 0.0 all-reduce.4.cloned.1.call-start
  6.5 0.7 fusion.30
  7.3 3.2 %copy.8 = bf16[1,1024,1536]{1,2,0:T(8,128)(2,1)S(1)} copy(bf16[1,1024,1536]{2,1,0:T(8,128)(2,1)} %param.10) | data formatting | bytes 6291456 | tf_op args[0]
  10.5 2.0 gather_fusion
  12.4 0.0 copy-start.2
  12.4 2.1 fusion.14
  14.5 0.0 all-reduce.4.cloned.1.call-update
  14.6 0.0 all-reduce.6.cloned.1.call-start
  14.6 0.0 copy-done.2
  14.6 0.0 copy-start.6
  14.6 0.0 copy-start.4
  14.7 0.0 copy-start.5
  14.7 0.5 copy.9
  15.8 0.0 copy-done.6
  15.8 0.7 fusion.29
  16.5 73.7 %all-reduce.4.cloned.1.call-done = bf16[1024,256]{0,1:T(8,128)(2,1)} async-done(((bf16[1024,256]{0,1:T(8,128)(2,1)}), bf16[1024,256]{0,1:T(8,128)(2,1)}) %all-reduce.4.cloned.1.call-update) | async-done | bytes 524304 | tf_op jit(solution)/shard_map/psum | solution.py:48
  90.2 0.0 copy-done
  90.2 1.3 fusion.11
  91.5 27.2 %all-gather = bf16[1024,256]{0,1:T(8,128)(2,1)S(1)} all-gather(bf16[128,256]{0,1:T(8,128)(2,1)S(1)} %fusion.11), channel_id=2, replica_groups=mesh['scen'=4,'row'=8] {'row'}, dimensions={0}, use_global_device_ids=true | all-gather | bytes 589824 | tf_op jit(solution)/shard_map/all_gather | solution.py:52
  118.7 0.0 copy-done.4
  118.7 0.0 copy-done.5
  118.7 3.6 %fusion.8 = f32[1536,256]{0,1:T(8,128)S(1)} fusion(bf16[1024,256]{0,1:T(8,128)(2,1)S(1)} %all-gather, bf16[1,1024,1536]{2,1,0:T(8,128)(2,1)} %param.10, f32[1536,256]{0,1:T(8,128)S(1)} %copy.9, f32[1536]{0:T(1024)S(1)} %copy-done.5, s32[1536]{0:T(1024)S(1)} %iota_add_fusion, f32[]{:T(128)S(6)} %convert_element_type.24, f32[]{:T(128)} %fusion.29, ...), kind=kOutput, calls=%fused_computation.6 | convolution fusion | flops 807665664 | bytes 6829064 | tf_op jit(solution)/shard_map/snr,snc->src/dot_general | solution.py:59
  122.3 0.0 copy-start.1
  122.4 0.5 copy.10
  122.8 0.7 copy-done.1
  123.5 1.7 gather_fusion.1
  125.2 1.8 select_multiply_fusion
  127.0 0.0 all-reduce.6.cloned.1.call-update
  127.0 0.2 all-reduce.8.cloned.1.call-start
  127.2 0.5 all-reduce.8.cloned.1.call-update
  127.7 124.2 %all-reduce.6.cloned.1.call-done = f32[256,256]{1,0:T(8,128)} async-done(((f32[256,256]{1,0:T(8,128)}), f32[256,256]{1,0:T(8,128)}) %all-reduce.6.cloned.1.call-update) | async-done | bytes 262160 | tf_op jit(solution)/shard_map/psum | solution.py:62
  251.9 1.1 copy.11
  253.0 1.0 fusion.15
  254.1 0.1 copy.12
  254.2 11.7 %cholesky.44 = f32[128,128]{1,0:T(8,128)S(1)} custom-call(f32[128,128]{1,0:T(8,128)S(1)} %fusion.25), custom_call_target="Cholesky" | custom-call | tf_op jit(solution)/shard_map/jit(cholesky)/cholesky | solution.py:27
  265.9 0.7 compare_reduce_fusion.1
  266.6 0.6 fusion.19
  267.2 9.8 %custom-call.10 = f32[1,128,128]{1,2,0:T(8,128)S(1)} custom-call(f32[1,128,128]{2,1,0:T(8,128)S(1)} %fusion.19), custom_call_target="InvertDiagBlocksLowerTriangular" | custom-call | tf_op jit(solution)/shard_map/triangular_solve/custom-call.0 | solution.py:34
  277.0 0.4 fusion.17
  277.4 0.3 fusion.27
  277.7 0.1 copy.14
  277.8 11.7 %cholesky.55 = f32[128,128]{1,0:T(8,128)S(1)} custom-call(f32[128,128]{1,0:T(8,128)S(1)} %fusion.22), custom_call_target="Cholesky" | custom-call | tf_op jit(solution)/shard_map/jit(cholesky)/cholesky | solution.py:27
  289.6 0.7 compare_reduce_fusion
  290.3 0.6 fusion.20
  290.9 10.0 %custom-call.11 = f32[1,128,128]{1,2,0:T(8,128)S(1)} custom-call(f32[1,128,128]{2,1,0:T(8,128)S(1)} %fusion.20), custom_call_target="InvertDiagBlocksLowerTriangular" | custom-call | tf_op jit(solution)/shard_map/triangular_solve/custom-call.0 | solution.py:34
  300.9 0.0 all-reduce.8.cloned.1.call-done
  300.9 0.0 copy-start.3
  300.9 2.1 convolution_bitcast_fusion.1
  303.0 0.0 copy-done.3
  303.0 0.8 convolution_subtract_fusion
  303.9 0.8 convolution_bitcast_fusion
  304.7 0.1 pad_maximum_fusion
  304.8 1.6 copy.15
  (10 shorter events, 0.1 us)
Async XLA Ops:
  6.5 83.7 %copy-start = (bf16[1,128,1024]{2,1,0:T(8,128)(2,1)S(1)}, bf16[1,128,1024]{2,1,0:T(8,128)(2,1)}, u32[]{:S(2)}) copy-start(bf16[1,128,1024]{2,1,0:T(8,128)(2,1)} %param.11) | copy-start | bytes 786436
  6.5 83.6 %all-reduce.4.cloned.1.call-start = ((), (), s32[]{:S(2)}) async-start(), calls=%async_computation | async-start | bytes 1048576 | tf_op jit(solution)/shard_map/psum | solution.py:48
  12.4 2.2 copy-start.2
  14.6 237.4 %all-reduce.6.cloned.1.call-start = ((), (), s32[]{:S(2)}) async-start(), calls=%async_computation.1 | async-start | bytes 524288 | tf_op jit(solution)/shard_map/psum | solution.py:62
  14.6 1.2 copy-start.6
  14.6 104.1 %copy-start.4 = (s32[256]{0:T(256)S(1)}, s32[256]{0:T(256)}, u32[]{:S(2)}) copy-start(s32[256]{0:T(256)} %param.14) | copy-start | bytes 3076
  14.7 104.1 %copy-start.5 = (f32[1536]{0:T(1024)S(1)}, f32[1536]{0:T(1024)}, u32[]{:S(2)}) copy-start(f32[1536]{0:T(1024)} %param.13) | copy-start | bytes 18436
  122.3 1.1 copy-start.1
  127.0 173.9 %all-reduce.8.cloned.1.call-start = ((), (), s32[]{:S(2)}) async-start(), calls=%async_computation.2 | async-start | bytes 3145728 | tf_op jit(solution)/shard_map/psum | solution.py:63
  300.9 2.1 copy-start.3
Sparse Core Ops, SparseCore 0:
  14.7 75.4 all-reduce.3
  127.1 124.8 all-reduce.5
  254.3 42.0 all-reduce.7
where the time goes:
time: 313 us
  waiting for transfers between devices  198 us (63%)
  other arithmetic  52.3 us (17%)
  blocking collectives  27.2 us (9%)
  between operations  14 us (4%)
  local copies, waits for them, and re-layouts  11.3 us (4%)
  matrix products  9.39 us (3%)
    psum x1, waiting for transfers between devices, per_device(): diag_block = lax.psum(own_block, ('scen', 'row'))  124 us
    psum x1, waiting for transfers between devices, per_device(): columns = lax.psum(picked, 'row').astype(jnp.float32).astype(jnp.bfloat16)  73.7 us
    all_gather x1, blocking collectives, per_device(): solved = lax.all_gather(own_solved, 'row', axis=1, tiled=True)  27.2 us
    another operation x6, other arithmetic, factorize(): panel_chol = jnp.linalg.cholesky(block_cols[low_col:high_col, :])  24.8 us
    another operation x4, other arithmetic, factorize(): lax.linalg.triangular_solve(panel_chol, row_cols, left_side=False, lower=...  21 us
  transfers between devices with their start and end apart: 3, of which 2 were waited for; matrix products, arithmetic and copies ran while one was open for 16% of the time, Pallas kernels for 0%

commit v1 on v0

v1 whole, which is shorter than its diff:
```python
import functools

import jax
import jax.numpy as jnp
from jax import lax
from jax.experimental import pallas as pl
from jax.experimental.pallas import tpu as pltpu
from jax.sharding import PartitionSpec as P

PANEL = 128
MESH = pl.DeviceIdType.MESH
HIGH = lax.Precision.HIGHEST
F32 = jnp.float32
BF16 = jnp.bfloat16
CHUNKS = 4


def factorize(symmetric, row_block):
    window = symmetric.shape[0]
    block_parts = []
    row_parts = []
    for low_col in range(0, window, PANEL):
        high_col = low_col + PANEL
        block_cols = symmetric[:, low_col:high_col]
        row_cols = row_block[:, low_col:high_col]
        if low_col > 0:
            earlier_block = jnp.concatenate(block_parts, axis=1)
            earlier_rows = jnp.concatenate(row_parts, axis=1)
            across = earlier_block[low_col:high_col, :]
            block_cols = block_cols - jnp.dot(earlier_block, across.T, precision=HIGH)
            row_cols = row_cols - jnp.dot(earlier_rows, across.T, precision=HIGH)
        panel_chol = jnp.linalg.cholesky(block_cols[low_col:high_col, :])
        block_parts.append(
            lax.linalg.triangular_solve(
                panel_chol, block_cols, left_side=False, lower=True, transpose_a=True
            )
        )
        row_parts.append(
            lax.linalg.triangular_solve(
                panel_chol, row_cols, left_side=False, lower=True, transpose_a=True
            )
        )
    return jnp.concatenate(row_parts, axis=1)


def flip(index, bit):
    return index + bit * (1 - 2 * ((index // bit) % 2))


def toggle(index, mask):
    bit = 1
    while bit <= mask:
        if mask & bit:
            index = flip(index, bit)
        bit *= 2
    return index


def bits_down(count):
    bits = []
    bit = count // 2
    while bit >= 1:
        bits.append(bit)
        bit //= 2
    return bits


def low_bit(mask):
    return mask & -mask


def gather_blocks(held, me, count, send_sem, recv_sem):
    bits = bits_down(count)

    def copy(mask, bit):
        owner = toggle(me, mask)
        return pltpu.make_async_remote_copy(
            src_ref=held.at[owner],
            dst_ref=held.at[owner],
            send_sem=send_sem.at[mask + bit],
            recv_sem=recv_sem.at[mask + bit],
            device_id={"row": flip(me, bit)},
            device_id_type=MESH,
        )

    order = [0]
    for bit in bits:
        order += [mask + bit for mask in list(order)]
    sent = []
    for mask in order:
        if mask:
            landed = pltpu.make_async_remote_copy(
                src_ref=held.at[toggle(me, mask)],
                dst_ref=held.at[toggle(me, mask)],
                send_sem=send_sem.at[mask],
                recv_sem=recv_sem.at[mask],
                device_id={"row": flip(me, low_bit(mask))},
                device_id_type=MESH,
            )
            landed.wait_recv()
        for bit in bits:
            if mask == 0 or bit < low_bit(mask):
                one = copy(mask, bit)
                one.start()
                sent.append(one)
    return sent


def schur_kernel(
    n_scen, n_row,
    pv_row, pv_col, prob, asg, b_ref, k_ref, base,
    diag, h_ref,
    onehot, picked, parts, columns, solved, fpick, fparts, fall, bt,
    t_own, t_in, t_sum, out_half, in_half, mine, y_in,
    rs_send, rs_recv, fs_send, fs_recv, agc_send, agc_recv, agf_send, agf_recv,
    ags_send, ags_recv, t_send, t_recv, c_send, c_recv, y_send, y_recv,
    g_send, g_recv,
):
    scen = lax.axis_index("scen")
    row = lax.axis_index("row")
    depth = picked.shape[1]
    rows, window = base.shape
    barrier = pltpu.get_barrier_semaphore()
    scen_bits = bits_down(n_scen)[::-1]
    for step in range(1, n_row):
        pl.semaphore_signal(
            barrier, inc=1, device_id={"row": (row + step) % n_row}, device_id_type=MESH
        )
    for bit in scen_bits:
        pl.semaphore_signal(
            barrier, inc=1, device_id={"scen": flip(scen, bit)}, device_id_type=MESH
        )

    first = row * rows
    local = pv_row[...] - first
    onehot[...] = jnp.where(
        lax.broadcasted_iota(jnp.int32, (rows, window), 0) == local, 1.0, 0.0
    ).astype(BF16)

    fgroups = fpick.shape[0]
    del fgroups
    frows = fpick.shape[0] * fpick.shape[1]
    groups = window // frows
    fstart = pl.multiple_of((scen % groups) * frows, 8)
    flocal = pv_col[pl.ds(fstart, frows), :] - first
    fhot = jnp.where(
        lax.broadcasted_iota(jnp.int32, (frows, rows), 1) == flocal, 1.0, 0.0
    ).astype(F32)

    pl.semaphore_wait(barrier, n_row - 1 + len(scen_bits))

    def pick(dst):
        start = pl.multiple_of(dst * depth, depth)
        block = jnp.dot(
            b_ref[pl.ds(start, depth), :], onehot[...], preferred_element_type=F32
        )
        return block.astype(BF16)

    def rs_copy(src, dst_ref, send, recv, dst, slot_send, slot_recv):
        return pltpu.make_async_remote_copy(
            src_ref=src,
            dst_ref=dst_ref,
            send_sem=send.at[slot_send],
            recv_sem=recv.at[slot_recv],
            device_id={"row": dst},
            device_id_type=MESH,
        )

    def send_pick(step, carry):
        dst = (row + step) % n_row
        picked[dst] = pick(dst)
        rs_copy(picked.at[dst], parts.at[row], rs_send, rs_recv, dst, dst, row).start()
        return carry

    lax.fori_loop(1, n_row, send_pick, 0)
    parts[row] = pick(row)

    fpick[...] = jnp.dot(
        fhot, base[...], preferred_element_type=F32, precision=HIGH
    ).reshape(fpick.shape)
    for step in range(1, n_row):
        dst = (row + step) % n_row
        rs_copy(fpick.at[dst], fparts.at[row], fs_send, fs_recv, dst, dst, row).start()
    fparts[row] = fpick[row]

    def turn(tile, carry):
        start = pl.multiple_of(tile * PANEL, PANEL)
        bt[pl.ds(start, PANEL), :] = b_ref[:, pl.ds(start, PANEL)].T
        return carry

    lax.fori_loop(0, rows // PANEL, turn, 0)

    for step in range(1, n_row):
        src = (row + n_row - step) % n_row
        rs_copy(picked.at[src], parts.at[src], rs_send, rs_recv, src, src, src).wait_recv()
    total = parts[0].astype(F32)
    for slot in range(1, n_row):
        total = total + parts[slot].astype(F32)
    columns[row] = total.astype(BF16)
    sent = gather_blocks(columns, row, n_row, agc_send, agc_recv)

    own = jnp.dot(
        k_ref[...],
        columns[...].reshape(n_row * depth, window),
        preferred_element_type=F32,
    )
    solved[row] = own.astype(BF16)
    sent += gather_blocks(solved, row, n_row, ags_send, ags_recv)

    for step in range(1, n_row):
        src = (row + n_row - step) % n_row
        rs_copy(fpick.at[src], fparts.at[src], fs_send, fs_recv, src, src, src).wait_recv()
    ftotal = fparts[0]
    for slot in range(1, n_row):
        ftotal = ftotal + fparts[slot]
    fall[row] = ftotal
    sent += gather_blocks(fall, row, n_row, agf_send, agf_recv)

    match = lax.broadcasted_iota(jnp.int32, prob.shape, 1) == asg[...]
    weight = jnp.sum(jnp.where(match, prob[...], 0.0), axis=1, keepdims=True)

    t_own[...] = weight * lax.dot_general(
        columns[...].reshape(n_row * depth, window),
        solved[...].reshape(n_row * depth, window),
        (((0,), (0,)), ((), ())),
        preferred_element_type=F32,
    )
    keep = jnp.where(scen < groups, 1.0, 0.0)
    t_own[pl.ds(fstart, frows), :] += fall[...].reshape(frows, window) * keep

    def t_copy(index, bit, src):
        return pltpu.make_async_remote_copy(
            src_ref=src,
            dst_ref=t_in.at[index],
            send_sem=t_send.at[index],
            recv_sem=t_recv.at[index],
            device_id={"scen": flip(scen, bit)},
            device_id_type=MESH,
        )

    def t_src(index):
        return t_own if index == 0 else t_sum.at[index - 1]

    t_copy(0, scen_bits[0], t_own).start()

    half = rows // 2
    chunk = half // CHUNKS
    core = scen % 2

    def term(which, part):
        start = pl.multiple_of(which * half + part * chunk, 8)
        return weight * jnp.dot(
            bt[pl.ds(start, chunk), :],
            solved[...].reshape(n_row * depth, window),
            preferred_element_type=F32,
        )

    def c_copy(part):
        return pltpu.make_async_remote_copy(
            src_ref=out_half.at[part],
            dst_ref=in_half.at[part],
            send_sem=c_send.at[part],
            recv_sem=c_recv.at[part],
            device_id={"scen": flip(scen, 1)},
            device_id_type=MESH,
        )

    def y_copy(index, bit, part):
        return pltpu.make_async_remote_copy(
            src_ref=mine.at[index, part],
            dst_ref=y_in.at[index, part],
            send_sem=y_send.at[index, part],
            recv_sem=y_recv.at[index, part],
            device_id={"scen": flip(scen, bit)},
            device_id_type=MESH,
        )

    for part in range(CHUNKS):
        out_half[part] = term(1 - core, part)
        c_copy(part).start()

    def t_step(index):
        copy = t_copy(index, scen_bits[index], t_src(index))
        copy.wait_recv()
        t_sum[index] = t_src(index)[...] + t_in[index]
        if index + 1 < len(scen_bits):
            t_copy(index + 1, scen_bits[index + 1], t_sum.at[index]).start()

    for part in range(CHUNKS):
        mine[0, part] = term(core, part)
    t_step(0)
    y_bits = scen_bits[1:]
    for part in range(CHUNKS):
        c_copy(part).wait_recv()
        mine[0, part] += in_half[part]
        y_copy(0, y_bits[0], part).start()
    for index in range(1, len(scen_bits)):
        t_step(index)
    whole = t_sum[len(scen_bits) - 1]
    diag[...] = 0.5 * (whole + whole.T)

    def g_copy(part):
        start = pl.multiple_of(core * half + part * chunk, 8)
        return pltpu.make_async_remote_copy(
            src_ref=mine.at[len(y_bits), part],
            dst_ref=h_ref.at[pl.ds(start, chunk), :],
            send_sem=g_send.at[part],
            recv_sem=g_recv.at[part],
            device_id={"scen": flip(scen, 1)},
            device_id_type=MESH,
        )

    for index, bit in enumerate(y_bits):
        for part in range(CHUNKS):
            y_copy(index, bit, part).wait_recv()
            total_part = mine[index, part] + y_in[index, part]
            start = pl.multiple_of(core * half + part * chunk, 8)
            if index + 1 == len(y_bits):
                total_part = total_part + base[pl.ds(start, chunk), :]
            mine[index + 1, part] = total_part
            if index + 1 < len(y_bits):
                y_copy(index + 1, y_bits[index + 1], part).start()
            else:
                h_ref[pl.ds(start, chunk), :] = total_part
                g_copy(part).start()
    for part in range(CHUNKS):
        g_copy(part).wait()

    for one in sent:
        one.wait_send()
    for step in range(1, n_row):
        dst = (row + step) % n_row
        rs_copy(picked.at[dst], parts.at[row], rs_send, rs_recv, dst, dst, row).wait_send()
        rs_copy(fpick.at[dst], fparts.at[row], fs_send, fs_recv, dst, dst, row).wait_send()
    for index, bit in enumerate(scen_bits):
        t_copy(index, bit, t_src(index)).wait_send()
    for part in range(CHUNKS):
        c_copy(part).wait_send()
        for index, bit in enumerate(y_bits):
            y_copy(index, bit, part).wait_send()


def per_device(
    n_scen, n_row,
    borders, kkt_inverse, first_section, barrier, panel_vars, probability, assignment,
):
    rows, window = first_section.shape
    depth = kkt_inverse.shape[1]
    full = kkt_inverse.shape[2]
    first_row = lax.axis_index("row") * rows
    hits = jnp.arange(rows, dtype=jnp.int32)[:, None] + first_row == panel_vars[None, :]
    base = first_section + jnp.where(hits, barrier[:, None], 0.0)
    groups = max(1, min(n_scen, window // (8 * n_row)))
    frow = window // groups // n_row
    stages = n_scen.bit_length() - 1
    half_chunk = rows // 2 // CHUNKS
    dma = pltpu.SemaphoreType.DMA
    vmem = pl.BlockSpec(memory_space=pltpu.VMEM)
    diag, schur = pl.pallas_call(
        functools.partial(schur_kernel, n_scen, n_row),
        out_shape=(
            jax.ShapeDtypeStruct((window, window), F32),
            jax.ShapeDtypeStruct((rows, window), F32),
        ),
        in_specs=[vmem] * 7,
        out_specs=(vmem, vmem),
        scratch_shapes=[
            pltpu.VMEM((rows, window), BF16),
            pltpu.VMEM((n_row, depth, window), BF16),
            pltpu.VMEM((n_row, depth, window), BF16),
            pltpu.VMEM((n_row, depth, window), BF16),
            pltpu.VMEM((n_row, depth, window), BF16),
            pltpu.VMEM((n_row, frow, window), F32),
            pltpu.VMEM((n_row, frow, window), F32),
            pltpu.VMEM((n_row, frow, window), F32),
            pltpu.VMEM((rows, full), BF16),
            pltpu.VMEM((window, window), F32),
            pltpu.VMEM((stages, window, window), F32),
            pltpu.VMEM((stages, window, window), F32),
            pltpu.VMEM((CHUNKS, half_chunk, window), F32),
            pltpu.VMEM((CHUNKS, half_chunk, window), F32),
            pltpu.VMEM((stages, CHUNKS, half_chunk, window), F32),
            pltpu.VMEM((stages - 1, CHUNKS, half_chunk, window), F32),
            *[dma((n_row,))] * 10,
            dma((stages,)), dma((stages,)),
            dma((CHUNKS,)), dma((CHUNKS,)),
            dma((stages - 1, CHUNKS)), dma((stages - 1, CHUNKS)),
            dma((CHUNKS,)), dma((CHUNKS,)),
        ],
        compiler_params=pltpu.CompilerParams(collective_id=0, has_side_effects=True),
    )(
        panel_vars[None, :], panel_vars[:, None], probability[None, :],
        assignment[:, None], borders[0], kkt_inverse[0], base,
    )
    return factorize(diag, schur)


def solution(mesh):
    placed = (
        P("scen", None, "row"),
        P("scen", "row", None),
        P("row", None),
        P("row"),
        P(),
        P(),
        P("scen"),
    )
    return jax.shard_map(
        functools.partial(per_device, mesh.shape["scen"], mesh.shape["row"]),
        mesh=mesh, in_specs=placed, out_specs=P("row", None), check_vma=False,
    )
```

time: 313 us -> 146 us (0.47)
  waiting for transfers between devices: 198 us -> 0 us
  Pallas kernels: 0 us -> 86.5 us
  blocking collectives: 27.2 us -> 0 us
  between operations: 14 us -> 0.83 us
  local copies, waits for them, and re-layouts: 11.3 us -> 4.47 us
  matrix products: 9.39 us -> 4.59 us
    psum x3 -> x0, waiting for transfers between devices: 198 us -> none  [the longest x1 124 us: per_device(): diag_block = lax.psum(own_block, ('scen', 'row'))]
    pallas_call x0 -> x1, Pallas kernels: none -> 86.5 us  [per_device(): pl.pallas_call(functools.partial(schur_kernel, n_scen, n_row), out_shape=...]
    all_gather x1 -> x0, blocking collectives: 27.2 us -> none  [per_device(): solved = lax.all_gather(own_solved, 'row', axis=1, tiled=True)]
    dot_general x4 -> x2, matrix products: 6.08 us -> 1.68 us  [the longest x1 1.41 us: factorize(): row_cols = row_cols - jnp.dot(earlier_rows, across.T, precision=HIGH)]
    unnamed x16 -> x2, local copies, waits for them, and re-layouts: 4.34 us -> 0.01 us
    gather x2 -> x0, local copies, waits for them, and re-layouts: 3.63 us -> none  [the longest x1 1.96 us: per_device(): jnp.take(borders, clipped, axis=2)]
    add x1 -> x2, other arithmetic: 0.01 us -> 3.28 us  [the longest x1 3.28 us: per_device(): base = first_section + jnp.where(hits, barrier[:, None], 0.0)]
  transfers between devices with their start and end apart: 3 -> 0, of which waited for: 2 -> 0; matrix products, arithmetic and copies ran while one was open for 16% -> 0% of each run, Pallas kernels for 0% -> 0%
where the time goes in v1:
time: 146 us
  Pallas kernels  86.5 us (59%)
  other arithmetic  49.3 us (34%)
  matrix products  4.59 us (3%)
  local copies, waits for them, and re-layouts  4.47 us (3%)
    pallas_call x1, Pallas kernels, per_device(): pl.pallas_call(functools.partial(schur_kernel, n_scen, n_row), out_shape=...  86.5 us
    another operation x6, other arithmetic, factorize(): panel_chol = jnp.linalg.cholesky(block_cols[low_col:high_col, :])  24.9 us
    another operation x4, other arithmetic, factorize(): lax.linalg.triangular_solve(panel_chol, row_cols, left_side=False, lower=...  20.9 us
    add x1, other arithmetic, per_device(): base = first_section + jnp.where(hits, barrier[:, None], 0.0)  3.28 us

profile of v1, /device:TPU:0, one launch (start us, length us, event | category | flops | bytes accessed | tf_op | source)
XLA Modules:
  0.0 145.7 jit_solution(9409945386516344740)
XLA Ops:
  0.7 1.5 %copy.14.pv_col = s32[256,1]{1,0:T(8,128)} copy(s32[256,1]{0,1:T(1,128)} %bitcast.38) | data formatting | bytes 2048 | tf_op jit(solution)/shard_map/broadcast_in_dim | solution.py:392
  2.1 3.3 %select_add_fusion.base = f32[1536,256]{1,0:T(8,128)} fusion(f32[1536,256]{1,0:T(8,128)} %param.12, f32[1536]{0:T(1024)} %param.13, s32[256]{0:T(256)} %param.14, s32[1536]{0:T(1024)S(1)} %iota_add_fusion), kind=kLoop, calls=%fused_computation.4 | loop fusion | flops 1179648 | bytes 3159040 | tf_op jit(solution)/shard_map/add | solution.py:352
  5.4 86.5 %shard_map.73 = (f32[256,256]{1,0:T(8,128)}, f32[1536,256]{1,0:T(8,128)}) custom-call(s32[1,256]{1,0:T(1,128)} %bitcast.39, s32[256,1]{1,0:T(8,128)} %copy.14.pv_col, f32[1,4]{1,0:T(1,128)} %bitcast.40, s32[1,1]{1,0:T(1,128)} %bitcast.35.asg, bf16[1024,1536]{1,0:T(8,128)(2,1)} %bitcast.36, bf16[128,1024]{1,0:T(8,128)(2,1)} %bitcast.37, ...), custom_call_target="tpu_custom_call" | custom-call | tf_op jit(solution)/shard_map/pallas_call | solution.py:359
  91.9 0.0 copy-start
  91.9 1.2 copy.15
  93.1 0.1 copy.16
  93.3 11.7 %cholesky.44 = f32[128,128]{1,0:T(8,128)S(1)} custom-call(f32[128,128]{1,0:T(8,128)S(1)} %fusion.9), custom_call_target="Cholesky" | custom-call | tf_op jit(solution)/shard_map/jit(cholesky)/cholesky | solution.py:32
  105.0 0.6 compare_reduce_fusion.1
  105.7 0.7 fusion.3
  106.3 9.8 %custom-call.10 = f32[1,128,128]{1,2,0:T(8,128)S(1)} custom-call(f32[1,128,128]{2,1,0:T(8,128)S(1)} %fusion.3), custom_call_target="InvertDiagBlocksLowerTriangular" | custom-call | tf_op jit(solution)/shard_map/triangular_solve/custom-call.0 | solution.py:39
  116.1 1.2 fusion.1
  117.3 0.3 fusion.11
  117.6 0.1 copy.19
  117.7 11.9 %cholesky.55 = f32[128,128]{1,0:T(8,128)S(1)} custom-call(f32[128,128]{1,0:T(8,128)S(1)} %fusion.6), custom_call_target="Cholesky" | custom-call | tf_op jit(solution)/shard_map/jit(cholesky)/cholesky | solution.py:32
  129.6 0.6 compare_reduce_fusion
  130.3 0.7 fusion.4
  131.0 9.8 %custom-call.11 = f32[1,128,128]{1,2,0:T(8,128)S(1)} custom-call(f32[1,128,128]{2,1,0:T(8,128)S(1)} %fusion.4), custom_call_target="InvertDiagBlocksLowerTriangular" | custom-call | tf_op jit(solution)/shard_map/triangular_solve/custom-call.0 | solution.py:39
  140.8 0.0 copy-done
  140.8 0.9 convolution_bitcast_fusion.1
  141.7 1.4 convolution_subtract_fusion
  143.1 0.9 convolution_bitcast_fusion
  143.9 0.1 pad_maximum_fusion
  144.1 1.6 %copy.20 = f32[1536,256]{1,0:T(8,128)} copy(f32[1536,256]{0,1:T(8,128)S(1)} %pad_maximum_fusion) | data formatting | bytes 3145728 | tf_op jit(solution)/shard_map/concatenate | solution.py:43
  (8 shorter events, 0.1 us)
Async XLA Ops:
  91.9 48.9 %copy-start = (f32[1536,256]{1,0:T(8,128)S(1)}, f32[1536,256]{1,0:T(8,128)}, u32[]{:S(2)}) copy-start(f32[1536,256]{1,0:T(8,128)} %get-tuple-element.10) | copy-start | bytes 4718596

commit v2 on v1

--- a/solution.py
+++ b/solution.py
@@ -13,34 +13,49 @@
 F32 = jnp.float32
 BF16 = jnp.bfloat16
 CHUNKS = 4
-
-
-def factorize(symmetric, row_block):
-    window = symmetric.shape[0]
-    block_parts = []
-    row_parts = []
-    for low_col in range(0, window, PANEL):
-        high_col = low_col + PANEL
-        block_cols = symmetric[:, low_col:high_col]
-        row_cols = row_block[:, low_col:high_col]
-        if low_col > 0:
-            earlier_block = jnp.concatenate(block_parts, axis=1)
-            earlier_rows = jnp.concatenate(row_parts, axis=1)
-            across = earlier_block[low_col:high_col, :]
-            block_cols = block_cols - jnp.dot(earlier_block, across.T, precision=HIGH)
-            row_cols = row_cols - jnp.dot(earlier_rows, across.T, precision=HIGH)
-        panel_chol = jnp.linalg.cholesky(block_cols[low_col:high_col, :])
-        block_parts.append(
-            lax.linalg.triangular_solve(
-                panel_chol, block_cols, left_side=False, lower=True, transpose_a=True
+SUB = 8
+BLOCK = 64
+
+
+def panel_inverse(block, size):
+    panel = block.shape[0]
+    sub = lax.broadcasted_iota(jnp.int32, (SUB, panel), 0)
+    lane = lax.broadcasted_iota(jnp.int32, (SUB, panel), 1)
+    left = [block[low:low + SUB, :] for low in range(0, panel, SUB)]
+    right = [
+        jnp.where(lane == sub + low, 1.0, 0.0) for low in range(0, panel, SUB)
+    ]
+    per = size // SUB
+    for base in range(0, panel // SUB, per):
+        for col in range(base * SUB, (base + per) * SUB):
+            own, line = col // SUB, col % SUB
+            scale = lax.rsqrt(left[own][line:line + 1, col:col + 1])
+            row_left = left[own][line:line + 1, :] * scale
+            row_right = right[own][line:line + 1, :] * scale
+            for tile in range(own, base + per):
+                factor = left[tile][:, col:col + 1] * scale
+                next_left = left[tile] - factor * row_left
+                next_right = right[tile] - factor * row_right
+                if tile == own:
+                    next_left = jnp.where(sub > line, next_left, left[tile])
+                    next_right = jnp.where(sub > line, next_right, right[tile])
+                    next_left = jnp.where(sub == line, row_left, next_left)
+                    next_right = jnp.where(sub == line, row_right, next_right)
+                left[tile], right[tile] = next_left, next_right
+        if base + per < panel // SUB:
+            upper = jnp.concatenate(left[base:base + per], axis=0)
+            both = jnp.concatenate(
+                [upper, jnp.concatenate(right[base:base + per], axis=0)], axis=1
             )
-        )
-        row_parts.append(
-            lax.linalg.triangular_solve(
-                panel_chol, row_cols, left_side=False, lower=True, transpose_a=True
+            change = lax.dot_general(
+                upper, both, (((0,), (0,)), ((), ())),
+                precision=HIGH, preferred_element_type=F32,
             )
-        )
-    return jnp.concatenate(row_parts, axis=1)
+            for tile in range(base + per, panel // SUB):
+                low = tile * SUB
+                left[tile] = left[tile] - change[low:low + SUB, :panel]
+                right[tile] = right[tile] - change[low:low + SUB, panel:]
+    return jnp.concatenate(right, axis=0)
 
 
 def flip(index, bit):
@@ -108,9 +123,9 @@
 
 def schur_kernel(
     n_scen, n_row,
-    pv_row, pv_col, prob, asg, b_ref, k_ref, base,
-    diag, h_ref,
-    onehot, picked, parts, columns, solved, fpick, fparts, fall, bt,
+    pv_row, prob, asg, bar_row, b_ref, k_ref, base,
+    f_ref,
+    h_ref, pv_col, onehot, picked, parts, columns, solved, fpick, fparts, fall, bt,
     t_own, t_in, t_sum, out_half, in_half, mine, y_in,
     rs_send, rs_recv, fs_send, fs_recv, agc_send, agc_recv, agf_send, agf_recv,
     ags_send, ags_recv, t_send, t_recv, c_send, c_recv, y_send, y_recv,
@@ -137,12 +152,11 @@
         lax.broadcasted_iota(jnp.int32, (rows, window), 0) == local, 1.0, 0.0
     ).astype(BF16)
 
-    fgroups = fpick.shape[0]
-    del fgroups
     frows = fpick.shape[0] * fpick.shape[1]
     groups = window // frows
     fstart = pl.multiple_of((scen % groups) * frows, 8)
-    flocal = pv_col[pl.ds(fstart, frows), :] - first
+    pv_col[...] = jnp.broadcast_to(pv_row[...], (SUB, window)).T
+    flocal = pv_col[pl.ds(fstart, frows), 0:1] - first
     fhot = jnp.where(
         lax.broadcasted_iota(jnp.int32, (frows, rows), 1) == flocal, 1.0, 0.0
     ).astype(F32)
@@ -175,8 +189,15 @@
     lax.fori_loop(1, n_row, send_pick, 0)
     parts[row] = pick(row)
 
-    fpick[...] = jnp.dot(
-        fhot, base[...], preferred_element_type=F32, precision=HIGH
+    bsel = jnp.dot(
+        jnp.broadcast_to(bar_row[...], (SUB, rows)), onehot[...].astype(F32),
+        preferred_element_type=F32, precision=HIGH,
+    )[0:1, :]
+    slot_row = lax.broadcasted_iota(jnp.int32, (frows, window), 0) + fstart
+    slot_col = lax.broadcasted_iota(jnp.int32, (frows, window), 1)
+    fpick[...] = (
+        jnp.dot(fhot, base[...], preferred_element_type=F32, precision=HIGH)
+        + jnp.where(slot_row == slot_col, bsel, 0.0)
     ).reshape(fpick.shape)
     for step in range(1, n_row):
         dst = (row + step) % n_row
@@ -297,7 +318,27 @@
     for index in range(1, len(scen_bits)):
         t_step(index)
     whole = t_sum[len(scen_bits) - 1]
-    diag[...] = 0.5 * (whole + whole.T)
+    symmetric = 0.5 * (whole + whole.T)
+    panels = window // PANEL
+    inverses, lowers = [], []
+
+    def matmul_t(lhs, rhs):
+        return lax.dot_general(
+            lhs, rhs, (((1,), (1,)), ((), ())),
+            precision=HIGH, preferred_element_type=F32,
+        )
+
+    def next_panel(index):
+        low = index * PANEL
+        block = symmetric[low:, low:low + PANEL]
+        for earlier in range(index):
+            rest = lowers[earlier][low - earlier * PANEL:, :]
+            block = block - matmul_t(rest, rest[:PANEL, :])
+        inverse = panel_inverse(block[:PANEL, :], BLOCK)
+        inverses.append(inverse)
+        lowers.append(matmul_t(block, inverse))
+
+    next_panel(0)
 
     def g_copy(part):
         start = pl.multiple_of(core * half + part * chunk, 8)
@@ -316,15 +357,36 @@
             total_part = mine[index, part] + y_in[index, part]
             start = pl.multiple_of(core * half + part * chunk, 8)
             if index + 1 == len(y_bits):
-                total_part = total_part + base[pl.ds(start, chunk), :]
+                total_part = total_part + (
+                    base[pl.ds(start, chunk), :]
+                    + onehot[pl.ds(start, chunk), :].astype(F32) * bsel
+                )
             mine[index + 1, part] = total_part
             if index + 1 < len(y_bits):
                 y_copy(index + 1, y_bits[index + 1], part).start()
             else:
                 h_ref[pl.ds(start, chunk), :] = total_part
                 g_copy(part).start()
+    for index in range(1, panels):
+        next_panel(index)
+
+    def finish(which, part):
+        start = pl.multiple_of(which * half + part * chunk, 8)
+        done = []
+        for index in range(panels):
+            low = index * PANEL
+            cols = h_ref[pl.ds(start, chunk), low:low + PANEL]
+            for earlier in range(index):
+                across = lowers[earlier][low - earlier * PANEL:, :][:PANEL, :]
+                cols = cols - matmul_t(done[earlier], across)
+            done.append(matmul_t(cols, inverses[index]))
+            f_ref[pl.ds(start, chunk), low:low + PANEL] = done[index]
+
+    for part in range(CHUNKS):
+        finish(core, part)
     for part in range(CHUNKS):
         g_copy(part).wait()
+        finish(1 - core, part)
 
     for one in sent:
         one.wait_send()
@@ -347,24 +409,20 @@
     rows, window = first_section.shape
     depth = kkt_inverse.shape[1]
     full = kkt_inverse.shape[2]
-    first_row = lax.axis_index("row") * rows
-    hits = jnp.arange(rows, dtype=jnp.int32)[:, None] + first_row == panel_vars[None, :]
-    base = first_section + jnp.where(hits, barrier[:, None], 0.0)
     groups = max(1, min(n_scen, window // (8 * n_row)))
     frow = window // groups // n_row
     stages = n_scen.bit_length() - 1
     half_chunk = rows // 2 // CHUNKS
     dma = pltpu.SemaphoreType.DMA
     vmem = pl.BlockSpec(memory_space=pltpu.VMEM)
-    diag, schur = pl.pallas_call(
+    return pl.pallas_call(
         functools.partial(schur_kernel, n_scen, n_row),
-        out_shape=(
-            jax.ShapeDtypeStruct((window, window), F32),
-            jax.ShapeDtypeStruct((rows, window), F32),
-        ),
+        out_shape=jax.ShapeDtypeStruct((rows, window), F32),
         in_specs=[vmem] * 7,
-        out_specs=(vmem, vmem),
+        out_specs=vmem,
         scratch_shapes=[
+            pltpu.VMEM((rows, window), F32),
+            pltpu.VMEM((window, SUB), jnp.int32),
             pltpu.VMEM((rows, window), BF16),
             pltpu.VMEM((n_row, depth, window), BF16),
             pltpu.VMEM((n_row, depth, window), BF16),
@@ -389,10 +447,9 @@
         ],
         compiler_params=pltpu.CompilerParams(collective_id=0, has_side_effects=True),
     )(
-        panel_vars[None, :], panel_vars[:, None], probability[None, :],
-        assignment[:, None], borders[0], kkt_inverse[0], base,
+        panel_vars[None, :], probability[None, :], assignment[:, None],
+        barrier[None, :], borders[0], kkt_inverse[0], first_section,
     )
-    return factorize(diag, schur)
 
 
 def solution(mesh):

time: 146 us -> 107 us (0.73)
  other arithmetic: 49.3 us -> 0 us
  Pallas kernels: 86.5 us -> 102 us
  matrix products: 4.59 us -> 0 us
    another operation x10 -> x0, other arithmetic: 45.9 us -> none  [the longest x6 24.9 us: factorize(): panel_chol = jnp.linalg.cholesky(block_cols[low_col:high_col, :])]
    pallas_call x1, Pallas kernels: 86.5 us -> 102 us  [per_device(): pl.pallas_call(functools.partial(schur_kernel, n_scen, n_row), out_shape=...]
    add x2 -> x0, other arithmetic: 3.28 us -> none  [the longest x1 3.28 us: per_device(): base = first_section + jnp.where(hits, barrier[:, None], 0.0)]
    another operation x3 -> x0, matrix products: 2.91 us -> none  [the longest x2 1.74 us: factorize(): lax.linalg.triangular_solve(panel_chol, row_cols, left_side=False, lower=...]
    unnamed x2 -> x1, local copies, waits for them, and re-layouts: 0.01 us -> 2.65 us
    dot_general x2 -> x0, matrix products: 1.68 us -> none  [the longest x1 1.41 us: factorize(): row_cols = row_cols - jnp.dot(earlier_rows, across.T, precision=HIGH)]
    concatenate x1 -> x0, local copies, waits for them, and re-layouts: 1.61 us -> none  [factorize(): return jnp.concatenate(row_parts, axis=1)]
where the time goes in v2:
time: 107 us
  Pallas kernels  102 us (95%)
  local copies, waits for them, and re-layouts  3.95 us (4%)
    pallas_call x1, Pallas kernels, per_device(): pl.pallas_call(functools.partial(schur_kernel, n_scen, n_row), out_shape=...  102 us
    unnamed x1, local copies, waits for them, and re-layouts  2.65 us

profile of v2, /device:TPU:0, one launch (start us, length us, event | category | flops | bytes accessed | tf_op | source)
XLA Modules:
  0.0 106.7 jit_solution(7737479484581180362)
XLA Ops:
  0.7 1.3 %broadcast_in_dim.15.bar_row = f32[1,1536]{1,0:T(1,128)} reshape(f32[1536]{0:T(1024)} %param.10) | data formatting | bytes 12288 | tf_op jit(solution)/shard_map/broadcast_in_dim | solution.py:451
  1.9 102.1 %shard_map.73 = f32[1536,256]{1,0:T(8,128)} custom-call(s32[1,256]{1,0:T(1,128)} %bitcast.8, f32[1,4]{1,0:T(1,128)} %bitcast.9, s32[1,1]{1,0:T(1,128)} %bitcast.5.asg, f32[1,1536]{1,0:T(1,128)} %broadcast_in_dim.15.bar_row, bf16[1024,1536]{1,0:T(8,128)(2,1)} %bitcast.6, bf16[128,1024]{1,0:T(8,128)(2,1)} %bitcast.7, f32[1536,256]{1,0:T(8,128)} %base.1), custom_call_target="tpu_custom_call" | custom-call | tf_op jit(solution)/shard_map/pallas_call | solution.py:418
  104.0 2.7 %copy.10 = f32[1536,256]{1,0:T(8,128)} copy(f32[1536,256]{1,0:T(8,128)} %shard_map.73) | data formatting | bytes 3145728

commit v3 on v2

--- a/solution.py
+++ b/solution.py
@@ -14,35 +14,74 @@
 BF16 = jnp.bfloat16
 CHUNKS = 4
 SUB = 8
-BLOCK = 64
+BLOCK = 32
+
+
+def small_factor(tile, first):
+    shape = tile.shape
+    spread = [
+        jnp.broadcast_to(tile[:, first + k:first + k + 1], shape) for k in range(SUB)
+    ]
+    cell = {
+        (i, k): jnp.broadcast_to(spread[k][i:i + 1, :], shape)
+        for k in range(SUB) for i in range(k, SUB)
+    }
+    scale, lower = [], {}
+    for j in range(SUB):
+        scale.append(lax.rsqrt(cell[j, j]))
+        for i in range(j + 1, SUB):
+            lower[i, j] = cell[i, j] * scale[j]
+        for k in range(j + 1, SUB):
+            for i in range(k, SUB):
+                cell[i, k] = cell[i, k] - lower[i, j] * lower[k, j]
+    inverse = {}
+    for j in range(SUB):
+        inverse[j, j] = scale[j]
+        for i in range(j + 1, SUB):
+            total = lower[i, j] * inverse[j, j]
+            for m in range(j + 1, i):
+                total = total + lower[i, m] * inverse[m, j]
+            inverse[i, j] = -(scale[i] * total)
+    return inverse
 
 
 def panel_inverse(block, size):
     panel = block.shape[0]
-    sub = lax.broadcasted_iota(jnp.int32, (SUB, panel), 0)
-    lane = lax.broadcasted_iota(jnp.int32, (SUB, panel), 1)
+    shape = (SUB, panel)
+    sub = lax.broadcasted_iota(jnp.int32, shape, 0)
+    lane = lax.broadcasted_iota(jnp.int32, shape, 1)
+    tiles = panel // SUB
     left = [block[low:low + SUB, :] for low in range(0, panel, SUB)]
-    right = [
-        jnp.where(lane == sub + low, 1.0, 0.0) for low in range(0, panel, SUB)
-    ]
+    right = [jnp.where(lane == sub + low, 1.0, 0.0) for low in range(0, panel, SUB)]
     per = size // SUB
-    for base in range(0, panel // SUB, per):
-        for col in range(base * SUB, (base + per) * SUB):
-            own, line = col // SUB, col % SUB
-            scale = lax.rsqrt(left[own][line:line + 1, col:col + 1])
-            row_left = left[own][line:line + 1, :] * scale
-            row_right = right[own][line:line + 1, :] * scale
-            for tile in range(own, base + per):
-                factor = left[tile][:, col:col + 1] * scale
-                next_left = left[tile] - factor * row_left
-                next_right = right[tile] - factor * row_right
-                if tile == own:
-                    next_left = jnp.where(sub > line, next_left, left[tile])
-                    next_right = jnp.where(sub > line, next_right, right[tile])
-                    next_left = jnp.where(sub == line, row_left, next_left)
-                    next_right = jnp.where(sub == line, row_right, next_right)
-                left[tile], right[tile] = next_left, next_right
-        if base + per < panel // SUB:
+    for base in range(0, tiles, per):
+        for own in range(base, base + per):
+            first = own * SUB
+            inverse = small_factor(left[own], first)
+            new_left = new_right = None
+            for k in range(SUB):
+                coeff = inverse[SUB - 1, k]
+                for i in range(SUB - 2, k - 1, -1):
+                    coeff = jnp.where(sub <= i, inverse[i, k], coeff)
+                if k:
+                    coeff = jnp.where(sub < k, 0.0, coeff)
+                add_left = coeff * left[own][k:k + 1, :]
+                add_right = coeff * right[own][k:k + 1, :]
+                new_left = add_left if k == 0 else new_left + add_left
+                new_right = add_right if k == 0 else new_right + add_right
+            for tile in range(own + 1, base + per):
+                spread = [
+                    jnp.broadcast_to(left[tile][:, first + m:first + m + 1], shape)
+                    for m in range(SUB)
+                ]
+                for k in range(SUB):
+                    factor = spread[0] * inverse[k, 0]
+                    for m in range(1, k + 1):
+                        factor = factor + spread[m] * inverse[k, m]
+                    left[tile] = left[tile] - factor * new_left[k:k + 1, :]
+                    right[tile] = right[tile] - factor * new_right[k:k + 1, :]
+            left[own], right[own] = new_left, new_right
+        if base + per < tiles:
             upper = jnp.concatenate(left[base:base + per], axis=0)
             both = jnp.concatenate(
                 [upper, jnp.concatenate(right[base:base + per], axis=0)], axis=1
@@ -51,7 +90,7 @@
                 upper, both, (((0,), (0,)), ((), ())),
                 precision=HIGH, preferred_element_type=F32,
             )
-            for tile in range(base + per, panel // SUB):
+            for tile in range(base + per, tiles):
                 low = tile * SUB
                 left[tile] = left[tile] - change[low:low + SUB, :panel]
                 right[tile] = right[tile] - change[low:low + SUB, panel:]
@@ -84,16 +123,16 @@
     return mask & -mask
 
 
-def gather_blocks(held, me, count, send_sem, recv_sem):
+def gather_blocks(arrays, me, count):
     bits = bits_down(count)
 
-    def copy(mask, bit):
-        owner = toggle(me, mask)
+    def copy(array, owner, mask, bit):
+        held, send_sem, recv_sem = array
         return pltpu.make_async_remote_copy(
             src_ref=held.at[owner],
             dst_ref=held.at[owner],
-            send_sem=send_sem.at[mask + bit],
-            recv_sem=recv_sem.at[mask + bit],
+            send_sem=send_sem.at[mask],
+            recv_sem=recv_sem.at[mask],
             device_id={"row": flip(me, bit)},
             device_id_type=MESH,
         )
@@ -103,30 +142,24 @@
         order += [mask + bit for mask in list(order)]
     sent = []
     for mask in order:
-        if mask:
-            landed = pltpu.make_async_remote_copy(
-                src_ref=held.at[toggle(me, mask)],
-                dst_ref=held.at[toggle(me, mask)],
-                send_sem=send_sem.at[mask],
-                recv_sem=recv_sem.at[mask],
-                device_id={"row": flip(me, low_bit(mask))},
-                device_id_type=MESH,
-            )
-            landed.wait_recv()
-        for bit in bits:
-            if mask == 0 or bit < low_bit(mask):
-                one = copy(mask, bit)
-                one.start()
-                sent.append(one)
+        for array in arrays:
+            owner = toggle(me, mask)
+            if mask:
+                copy(array, owner, mask, low_bit(mask)).wait_recv()
+            for bit in bits:
+                if mask == 0 or bit < low_bit(mask):
+                    one = copy(array, owner, mask + bit, bit)
+                    one.start()
+                    sent.append(one)
     return sent
 
 
 def schur_kernel(
     n_scen, n_row,
     pv_row, prob, asg, bar_row, b_ref, k_ref, base,
-    f_ref,
-    h_ref, pv_col, onehot, picked, parts, columns, solved, fpick, fparts, fall, bt,
-    t_own, t_in, t_sum, out_half, in_half, mine, y_in,
+    h_ref, m_ref,
+    pv_col, onehot, picked, parts, columns, solved, fpick, fparts, fall, bt,
+    t_own, t_in, t_sum, t_all, out_half, in_half, mine, y_in,
     rs_send, rs_recv, fs_send, fs_recv, agc_send, agc_recv, agf_send, agf_recv,
     ags_send, ags_recv, t_send, t_recv, c_send, c_recv, y_send, y_recv,
     g_send, g_recv,
@@ -190,7 +223,7 @@
     parts[row] = pick(row)
 
     bsel = jnp.dot(
-        jnp.broadcast_to(bar_row[...], (SUB, rows)), onehot[...].astype(F32),
+        jnp.broadcast_to(bar_row[...].reshape(1, rows), (SUB, rows)), onehot[...].astype(F32),
         preferred_element_type=F32, precision=HIGH,
     )[0:1, :]
     slot_row = lax.broadcasted_iota(jnp.int32, (frows, window), 0) + fstart
@@ -218,16 +251,6 @@
     for slot in range(1, n_row):
         total = total + parts[slot].astype(F32)
     columns[row] = total.astype(BF16)
-    sent = gather_blocks(columns, row, n_row, agc_send, agc_recv)
-
-    own = jnp.dot(
-        k_ref[...],
-        columns[...].reshape(n_row * depth, window),
-        preferred_element_type=F32,
-    )
-    solved[row] = own.astype(BF16)
-    sent += gather_blocks(solved, row, n_row, ags_send, ags_recv)
-
     for step in range(1, n_row):
         src = (row + n_row - step) % n_row
         rs_copy(fpick.at[src], fparts.at[src], fs_send, fs_recv, src, src, src).wait_recv()
@@ -235,7 +258,18 @@
     for slot in range(1, n_row):
         ftotal = ftotal + fparts[slot]
     fall[row] = ftotal
-    sent += gather_blocks(fall, row, n_row, agf_send, agf_recv)
+    sent = gather_blocks(
+        [(columns, agc_send, agc_recv), (fall, agf_send, agf_recv)], row, n_row
+    )
+
+    own = jnp.dot(
+        k_ref[...],
+        columns[...].reshape(n_row * depth, window),
+        preferred_element_type=F32,
+    )
+    solved[row] = own.astype(BF16)
+    sent += gather_blocks([(solved, ags_send, ags_recv)], row, n_row)
+
 
     match = lax.broadcasted_iota(jnp.int32, prob.shape, 1) == asg[...]
     weight = jnp.sum(jnp.where(match, prob[...], 0.0), axis=1, keepdims=True)
@@ -249,25 +283,32 @@
     keep = jnp.where(scen < groups, 1.0, 0.0)
     t_own[pl.ds(fstart, frows), :] += fall[...].reshape(frows, window) * keep
 
-    def t_copy(index, bit, src):
+    core = scen % 2
+    t_half = window // 2
+    t_mine = pl.multiple_of(core * t_half, 8)
+    t_other = pl.multiple_of((1 - core) * t_half, 8)
+
+    def t_copy(index):
+        if index == 0:
+            src, dst = t_own.at[pl.ds(t_other, t_half), :], t_in.at[0]
+        elif index < len(scen_bits):
+            src, dst = t_sum.at[index - 1], t_in.at[index]
+        else:
+            src = t_sum.at[index - 1]
+            dst = t_all.at[pl.ds(t_mine, t_half), :]
         return pltpu.make_async_remote_copy(
             src_ref=src,
-            dst_ref=t_in.at[index],
+            dst_ref=dst,
             send_sem=t_send.at[index],
             recv_sem=t_recv.at[index],
-            device_id={"scen": flip(scen, bit)},
+            device_id={"scen": flip(scen, (scen_bits + [1])[index])},
             device_id_type=MESH,
         )
 
-    def t_src(index):
-        return t_own if index == 0 else t_sum.at[index - 1]
-
-    t_copy(0, scen_bits[0], t_own).start()
+    t_copy(0).start()
 
     half = rows // 2
     chunk = half // CHUNKS
-    core = scen % 2
-
     def term(which, part):
         start = pl.multiple_of(which * half + part * chunk, 8)
         return weight * jnp.dot(
@@ -301,11 +342,12 @@
         c_copy(part).start()
 
     def t_step(index):
-        copy = t_copy(index, scen_bits[index], t_src(index))
-        copy.wait_recv()
-        t_sum[index] = t_src(index)[...] + t_in[index]
-        if index + 1 < len(scen_bits):
-            t_copy(index + 1, scen_bits[index + 1], t_sum.at[index]).start()
+        t_copy(index).wait_recv()
+        before = t_own[pl.ds(t_mine, t_half), :] if index == 0 else t_sum[index - 1]
+        t_sum[index] = before + t_in[index]
+        t_copy(index + 1).start()
+        if index + 1 == len(scen_bits):
+            t_all[pl.ds(t_mine, t_half), :] = t_sum[index]
 
     for part in range(CHUNKS):
         mine[0, part] = term(core, part)
@@ -317,7 +359,8 @@
         y_copy(0, y_bits[0], part).start()
     for index in range(1, len(scen_bits)):
         t_step(index)
-    whole = t_sum[len(scen_bits) - 1]
+    t_copy(len(scen_bits)).wait_recv()
+    whole = t_all[...]
     symmetric = 0.5 * (whole + whole.T)
     panels = window // PANEL
     inverses, lowers = [], []
@@ -351,42 +394,51 @@
             device_id_type=MESH,
         )
 
-    for index, bit in enumerate(y_bits):
-        for part in range(CHUNKS):
-            y_copy(index, bit, part).wait_recv()
-            total_part = mine[index, part] + y_in[index, part]
-            start = pl.multiple_of(core * half + part * chunk, 8)
-            if index + 1 == len(y_bits):
-                total_part = total_part + (
-                    base[pl.ds(start, chunk), :]
-                    + onehot[pl.ds(start, chunk), :].astype(F32) * bsel
-                )
-            mine[index + 1, part] = total_part
-            if index + 1 < len(y_bits):
-                y_copy(index + 1, y_bits[index + 1], part).start()
-            else:
-                h_ref[pl.ds(start, chunk), :] = total_part
-                g_copy(part).start()
+    def y_step(index, part):
+        y_copy(index, y_bits[index], part).wait_recv()
+        total_part = mine[index, part] + y_in[index, part]
+        start = pl.multiple_of(core * half + part * chunk, 8)
+        if index + 1 == len(y_bits):
+            total_part = total_part + (
+                base[pl.ds(start, chunk), :]
+                + onehot[pl.ds(start, chunk), :].astype(F32) * bsel
+            )
+        mine[index + 1, part] = total_part
+        if index + 1 < len(y_bits):
+            y_copy(index + 1, y_bits[index + 1], part).start()
+        else:
+            h_ref[pl.ds(start, chunk), :] = total_part
+            g_copy(part).start()
+
+    steps = [(index, part) for index in range(len(y_bits)) for part in range(CHUNKS)]
+    early = len(steps) // 2
+    for index, part in steps[:early]:
+        y_step(index, part)
     for index in range(1, panels):
         next_panel(index)
-
-    def finish(which, part):
-        start = pl.multiple_of(which * half + part * chunk, 8)
-        done = []
-        for index in range(panels):
-            low = index * PANEL
-            cols = h_ref[pl.ds(start, chunk), low:low + PANEL]
-            for earlier in range(index):
-                across = lowers[earlier][low - earlier * PANEL:, :][:PANEL, :]
-                cols = cols - matmul_t(done[earlier], across)
-            done.append(matmul_t(cols, inverses[index]))
-            f_ref[pl.ds(start, chunk), low:low + PANEL] = done[index]
-
-    for part in range(CHUNKS):
-        finish(core, part)
+    for index, part in steps[early:]:
+        y_step(index, part)
+
+    m_ref[...] = jnp.zeros_like(m_ref)
+    for index in range(panels):
+        low = index * PANEL
+        for earlier in range(index):
+            total = None
+            for middle in range(earlier, index):
+                across = lowers[middle][low - middle * PANEL:, :][:PANEL, :]
+                part = jnp.dot(
+                    across,
+                    m_ref[middle * PANEL:(middle + 1) * PANEL,
+                          earlier * PANEL:(earlier + 1) * PANEL],
+                    precision=HIGH, preferred_element_type=F32,
+                )
+                total = part if total is None else total + part
+            m_ref[low:low + PANEL, earlier * PANEL:(earlier + 1) * PANEL] = -jnp.dot(
+                inverses[index], total, precision=HIGH, preferred_element_type=F32
+            )
+        m_ref[low:low + PANEL, low:low + PANEL] = inverses[index]
     for part in range(CHUNKS):
         g_copy(part).wait()
-        finish(1 - core, part)
 
     for one in sent:
         one.wait_send()
@@ -394,8 +446,8 @@
         dst = (row + step) % n_row
         rs_copy(picked.at[dst], parts.at[row], rs_send, rs_recv, dst, dst, row).wait_send()
         rs_copy(fpick.at[dst], fparts.at[row], fs_send, fs_recv, dst, dst, row).wait_send()
-    for index, bit in enumerate(scen_bits):
-        t_copy(index, bit, t_src(index)).wait_send()
+    for index in range(len(scen_bits) + 1):
+        t_copy(index).wait_send()
     for part in range(CHUNKS):
         c_copy(part).wait_send()
         for index, bit in enumerate(y_bits):
@@ -415,13 +467,15 @@
     half_chunk = rows // 2 // CHUNKS
     dma = pltpu.SemaphoreType.DMA
     vmem = pl.BlockSpec(memory_space=pltpu.VMEM)
-    return pl.pallas_call(
+    schur, inverse = pl.pallas_call(
         functools.partial(schur_kernel, n_scen, n_row),
-        out_shape=jax.ShapeDtypeStruct((rows, window), F32),
+        out_shape=(
+            jax.ShapeDtypeStruct((rows, window), F32),
+            jax.ShapeDtypeStruct((window, window), F32),
+        ),
         in_specs=[vmem] * 7,
-        out_specs=vmem,
+        out_specs=(vmem, vmem),
         scratch_shapes=[
-            pltpu.VMEM((rows, window), F32),
             pltpu.VMEM((window, SUB), jnp.int32),
             pltpu.VMEM((rows, window), BF16),
             pltpu.VMEM((n_row, depth, window), BF16),
@@ -433,14 +487,15 @@
             pltpu.VMEM((n_row, frow, window), F32),
             pltpu.VMEM((rows, full), BF16),
             pltpu.VMEM((window, window), F32),
-            pltpu.VMEM((stages, window, window), F32),
-            pltpu.VMEM((stages, window, window), F32),
+            pltpu.VMEM((stages, window // 2, window), F32),
+            pltpu.VMEM((stages, window // 2, window), F32),
+            pltpu.VMEM((window, window), F32),
             pltpu.VMEM((CHUNKS, half_chunk, window), F32),
             pltpu.VMEM((CHUNKS, half_chunk, window), F32),
             pltpu.VMEM((stages, CHUNKS, half_chunk, window), F32),
             pltpu.VMEM((stages - 1, CHUNKS, half_chunk, window), F32),
             *[dma((n_row,))] * 10,
-            dma((stages,)), dma((stages,)),
+            dma((stages + 1,)), dma((stages + 1,)),
             dma((CHUNKS,)), dma((CHUNKS,)),
             dma((stages - 1, CHUNKS)), dma((stages - 1, CHUNKS)),
             dma((CHUNKS,)), dma((CHUNKS,)),
@@ -448,7 +503,11 @@
         compiler_params=pltpu.CompilerParams(collective_id=0, has_side_effects=True),
     )(
         panel_vars[None, :], probability[None, :], assignment[:, None],
-        barrier[None, :], borders[0], kkt_inverse[0], first_section,
+        barrier, borders[0], kkt_inverse[0], first_section,
+    )
+    return lax.dot_general(
+        schur, inverse, (((1,), (1,)), ((), ())),
+        precision=HIGH, preferred_element_type=F32,
     )
 
 

time: 107 us -> 76.7 us (0.72)
  Pallas kernels: 102 us -> 71.9 us
  matrix products: 0 us -> 4 us
  local copies, waits for them, and re-layouts: 3.95 us -> 0 us
    pallas_call x1, Pallas kernels: 102 us -> 71.9 us  [per_device(): pl.pallas_call(functools.partial(schur_kernel, n_scen, n_row), out_shape=...]
    dot_general x0 -> x1, matrix products: none -> 4 us  [per_device(): lax.dot_general(schur, inverse, (((1,), (1,)), ((), ())), precision=HIGH,...]
    unnamed x1 -> x0, local copies, waits for them, and re-layouts: 2.65 us -> none
    broadcast_in_dim x1 -> x0, local copies, waits for them, and re-layouts: 1.29 us -> none  [per_device(): barrier[None, :]]
where the time goes in v3:
time: 76.7 us; the launch traced here: 76.6 us
  Pallas kernels  71.9 us (94%)
  matrix products  4 us (5%)
    pallas_call x1, Pallas kernels, per_device(): pl.pallas_call(functools.partial(schur_kernel, n_scen, n_row), out_shape=...  71.9 us
    dot_general x1, matrix products, per_device(): lax.dot_general(schur, inverse, (((1,), (1,)), ((), ())), precision=HIGH,...  4 us

profile of v3, /device:TPU:0, one launch (start us, length us, event | category | flops | bytes accessed | tf_op | source)
XLA Modules:
  0.0 76.6 jit_solution(10684107219484454033)
XLA Ops:
  0.7 71.9 %shard_map.73 = (f32[1536,256]{1,0:T(8,128)}, f32[256,256]{1,0:T(8,128)}) custom-call(s32[1,256]{1,0:T(1,128)} %bitcast.10, f32[1,4]{1,0:T(1,128)} %bitcast.11, s32[1,1]{1,0:T(1,128)} %bitcast.7.asg, f32[1536]{0:T(1024)} %bar_row.1, bf16[1024,1536]{1,0:T(8,128)(2,1)} %bitcast.8, bf16[128,1024]{1,0:T(8,128)(2,1)} %bitcast.9, f32[1536,256]{1,0:T(8,128)} %base.1), custom_call_target="tpu_custom_call" | custom-call | tf_op jit(solution)/shard_map/pallas_call | solution.py:470
  72.6 4.0 %fusion = f32[1536,256]{1,0:T(8,128)} fusion(f32[1536,256]{1,0:T(8,128)} %get-tuple-element.7, f32[256,256]{1,0:T(8,128)} %get-tuple-element.8), kind=kOutput, calls=%fused_computation | convolution fusion | flops 1207959552 | bytes 3407872 | tf_op jit(solution)/shard_map/dot_general | solution.py:508

commit v4 on v3

--- a/solution.py
+++ b/solution.py
@@ -156,9 +156,9 @@
 
 def schur_kernel(
     n_scen, n_row,
-    pv_row, prob, asg, bar_row, b_ref, k_ref, base,
+    pv_row, prob, asg, bar_row, b_hbm, k_hbm, base_hbm,
     h_ref, m_ref,
-    pv_col, onehot, picked, parts, columns, solved, fpick, fparts, fall, bt,
+    b_ref, k_ref, base, load_sem, rest_sem, pv_col, onehot, picked, parts, columns, solved, fpick, fparts, fall, bt,
     t_own, t_in, t_sum, t_all, out_half, in_half, mine, y_in,
     rs_send, rs_recv, fs_send, fs_recv, agc_send, agc_recv, agf_send, agf_recv,
     ags_send, ags_recv, t_send, t_recv, c_send, c_recv, y_send, y_recv,
@@ -169,6 +169,17 @@
     depth = picked.shape[1]
     rows, window = base.shape
     barrier = pltpu.get_barrier_semaphore()
+
+    def load(block):
+        start = pl.multiple_of(block * depth, depth)
+        return pltpu.make_async_copy(
+            b_hbm.at[pl.ds(start, depth), :],
+            b_ref.at[pl.ds(start, depth), :],
+            load_sem.at[block],
+        )
+
+    base_load = pltpu.make_async_copy(base_hbm, base, rest_sem.at[0])
+    k_load = pltpu.make_async_copy(k_hbm, k_ref, rest_sem.at[1])
     scen_bits = bits_down(n_scen)[::-1]
     for step in range(1, n_row):
         pl.semaphore_signal(
@@ -178,6 +189,11 @@
         pl.semaphore_signal(
             barrier, inc=1, device_id={"scen": flip(scen, bit)}, device_id_type=MESH
         )
+
+    for step in range(1, n_row + 1):
+        load((row + step) % n_row).start()
+    base_load.start()
+    k_load.start()
 
     first = row * rows
     local = pv_row[...] - first
@@ -197,6 +213,7 @@
     pl.semaphore_wait(barrier, n_row - 1 + len(scen_bits))
 
     def pick(dst):
+        load(dst).wait()
         start = pl.multiple_of(dst * depth, depth)
         block = jnp.dot(
             b_ref[pl.ds(start, depth), :], onehot[...], preferred_element_type=F32
@@ -228,6 +245,7 @@
     )[0:1, :]
     slot_row = lax.broadcasted_iota(jnp.int32, (frows, window), 0) + fstart
     slot_col = lax.broadcasted_iota(jnp.int32, (frows, window), 1)
+    base_load.wait()
     fpick[...] = (
         jnp.dot(fhot, base[...], preferred_element_type=F32, precision=HIGH)
         + jnp.where(slot_row == slot_col, bsel, 0.0)
@@ -262,6 +280,7 @@
         [(columns, agc_send, agc_recv), (fall, agf_send, agf_recv)], row, n_row
     )
 
+    k_load.wait()
     own = jnp.dot(
         k_ref[...],
         columns[...].reshape(n_row * depth, window),
@@ -349,9 +368,9 @@
         if index + 1 == len(scen_bits):
             t_all[pl.ds(t_mine, t_half), :] = t_sum[index]
 
+    t_step(0)
     for part in range(CHUNKS):
         mine[0, part] = term(core, part)
-    t_step(0)
     y_bits = scen_bits[1:]
     for part in range(CHUNKS):
         c_copy(part).wait_recv()
@@ -473,9 +492,13 @@
             jax.ShapeDtypeStruct((rows, window), F32),
             jax.ShapeDtypeStruct((window, window), F32),
         ),
-        in_specs=[vmem] * 7,
+        in_specs=[vmem] * 4 + [pl.BlockSpec(memory_space=pl.ANY)] * 3,
         out_specs=(vmem, vmem),
         scratch_shapes=[
+            pltpu.VMEM((full, rows), BF16),
+            pltpu.VMEM((depth, full), BF16),
+            pltpu.VMEM((rows, window), F32),
+            dma((n_row,)), dma((2,)),
             pltpu.VMEM((window, SUB), jnp.int32),
             pltpu.VMEM((rows, window), BF16),
             pltpu.VMEM((n_row, depth, window), BF16),

time: 76.7 us -> 75 us (0.978)
  Pallas kernels: 71.9 us -> 70.1 us
    pallas_call x1, Pallas kernels: 71.9 us -> 70.1 us  [per_device(): pl.pallas_call(functools.partial(schur_kernel, n_scen, n_row), out_shape=...]
where the time goes in v4:
time: 75 us; the launch traced here: 74.8 us
  Pallas kernels  70.1 us (93%)
  matrix products  4 us (5%)
    pallas_call x1, Pallas kernels, per_device(): pl.pallas_call(functools.partial(schur_kernel, n_scen, n_row), out_shape=...  70.1 us
    dot_general x1, matrix products, per_device(): lax.dot_general(schur, inverse, (((1,), (1,)), ((), ())), precision=HIGH,...  4 us

profile of v4, /device:TPU:0, one launch (start us, length us, event | category | flops | bytes accessed | tf_op | source)
XLA Modules:
  0.0 74.8 jit_solution(9568969554742110443)
XLA Ops:
  0.7 70.1 %shard_map.73 = (f32[1536,256]{1,0:T(8,128)}, f32[256,256]{1,0:T(8,128)}) custom-call(s32[1,256]{1,0:T(1,128)} %bitcast.10, f32[1,4]{1,0:T(1,128)} %bitcast.11, s32[1,1]{1,0:T(1,128)} %bitcast.7.asg, f32[1536]{0:T(1024)} %bar_row.1, bf16[1024,1536]{1,0:T(8,128)(2,1)} %bitcast.8, bf16[128,1024]{1,0:T(8,128)(2,1)} %bitcast.9, f32[1536,256]{1,0:T(8,128)} %base_hbm.1), custom_call_target="tpu_custom_call" | custom-call | tf_op jit(solution)/shard_map/pallas_call | solution.py:489
  70.8 4.0 %fusion = f32[1536,256]{1,0:T(8,128)} fusion(f32[1536,256]{1,0:T(8,128)} %get-tuple-element.7, f32[256,256]{1,0:T(8,128)} %get-tuple-element.8), kind=kOutput, calls=%fused_computation | convolution fusion | flops 1207959552 | bytes 3407872 | tf_op jit(solution)/shard_map/dot_general | solution.py:531
